TPU v7x, 32 devices: a whole 2x2x4 slice. The times are simulated.
32 devices in a mesh: groups: 2 (over y), row: 4 (over x, core), col: 4 (over z).
Axes of the slice: x: 2, y: 2, z: 4, core: 2. Of those that a mesh axis runs over, the one named last changes fastest.
Arguments:
- slope_matrix: bfloat16 [1024, 1024], P(('groups', 'row'), 'col'), parts along dimension 0, may hold values from -0.3125 to 0.3125
- prior_matrix: bfloat16 [1024, 1024], P(('groups', 'row'), 'col'), parts along dimension 0, may hold values from -0.3125 to 0.3125
- slope_blocks: int32 [8, 8], P(('groups', 'row'), 'col'), parts along dimension 0, may hold values from 0 to 23, as said below
- prior_blocks: int32 [8, 8], P(('groups', 'row'), 'col'), parts along dimension 0, may hold values from 0 to 23, as said below
- weight_ids: int32 [512], P(('groups', 'row')), parts along dimension 0, may hold values from 0 to 15
- valid_mask: int32 [512], P(('groups', 'row')), parts along dimension 0, may hold values 0 or 1
- noise_weights: float32 [32], P('groups'), parts along dimension 0, may hold values from 0.25 to 4
- prior_weights: bfloat16 [1024], P(('groups', 'row')), parts along dimension 0, may hold values from 0.19921875 to 2
- frames: float32 [6144, 64], P(('groups', 'row', 'col')), parts along dimension 0, may hold values from -6 to 6
Outputs:
- gram_matrix: float32 [6144, 3072], P(('groups', 'row'), 'col'), parts along dimension 0
- applied: float32 [6144, 64], P(('groups', 'row', 'col')), parts along dimension 0
There are 2 independent parts, one for each index of `groups`. A program takes and returns all parts, laid end to end along the dimension named above; each array names one. Nothing has to cross between parts.
Inputs may be any that keep to these rules, and one draw needn't show every extreme that they name: `slope_blocks`: row i names, for each block-column set c (entries c * 2 to c * 2 + 1), 2 distinct actuator blocks of that set, c * 6 to c * 6 + 5, in the order in which their blocks are stored. `prior_blocks`: row i names, for each block-column set c (entries c * 2 to c * 2 + 1), 2 distinct actuator blocks of that set, c * 6 to c * 6 + 5, in the order in which their blocks are stored.
All inputs are finite; a program needn't handle non-finite values. No bound on the sum of `valid_mask` on one device may be relied on, other than what follows from the above.
Results may differ from a plain program's by a relative error of at most 0.007.
Values may be sent and summed in bfloat16 or wider, within the bound.
No kernel may reach another device: no remote copies, remote signals or barrier semaphores. Data moves between devices by JAX's collectives and lax.ppermute only.
A program may use at most 128 MiB of HBM per device.

v0:
```python
import functools

import jax
import jax.numpy as jnp
from jax import lax
from jax.experimental import pallas as pl
from jax.experimental.pallas import tpu as pltpu
from jax.sharding import PartitionSpec as P


VMEM = pl.BlockSpec(memory_space=pltpu.VMEM)
SMEM = pl.BlockSpec(memory_space=pltpu.SMEM)
F32 = jnp.float32
BF16 = jnp.bfloat16
EXTRA = 16
SMALL = pltpu.CompilerParams(vmem_limit_bytes=16 << 20)


def here(*values):
    return [pltpu.with_memory_space_constraint(v, pltpu.VMEM) for v in values]


def permute(value, n, source):
    pairs = []
    for r in range(n):
        for c in range(n):
            sr, sc = source(r, c)
            pairs.append((sr * n + sc, r * n + c))
    return lax.ppermute(value, ("row", "col"), pairs)


def pack_kernel(ab, slope, prior, ids_s, ids_p, wid, valid, pw, noise, frames, packed, sent):
    rows, width = slope.shape
    half = wid.shape[1]
    packed[0:rows, :] = slope[...]
    packed[rows : 2 * rows, :] = prior[...]
    picked = jnp.zeros((1, half), F32)
    for k in range(noise.shape[0]):
        picked = picked + jnp.where(wid[...] == k, noise[k], 0.0)
    picked = picked * valid[...].astype(F32)
    source = lax.broadcasted_iota(jnp.int32, (half, rows), 0)
    target = lax.broadcasted_iota(jnp.int32, (half, rows), 1)
    spread = jnp.where(target // 2 == source, 1.0, 0.0).astype(BF16)
    eight = jnp.broadcast_to(picked, (8, half)).astype(BF16)
    slope_w = jnp.dot(eight, spread, preferred_element_type=F32)[0:1]
    weights = jnp.concatenate([slope_w, pw[...].astype(F32)], axis=1)
    base = lax.axis_index("col") * ab
    row = lax.broadcasted_iota(jnp.int32, (EXTRA, width), 0)
    lane = lax.broadcasted_iota(jnp.int32, (EXTRA, width), 1)
    tile = jnp.where(row == 0, jnp.broadcast_to(weights, (EXTRA, width)), 0.0)
    for line, ids in ((1, ids_s), (2, ids_p)):
        for e in range(ids.shape[1]):
            here = (row == line) & (lane // rows == e)
            tile = jnp.where(here, (ids[0, e] - base).astype(F32), tile)
    packed[2 * rows :, :] = tile.astype(BF16)
    nf, per = frames.shape
    sent[...] = jnp.concatenate([frames[...], jnp.zeros((nf, width - per), F32)], axis=1).astype(BF16)


def info(block, rows, which):
    tile = block[2 * rows : 2 * rows + EXTRA, :].astype(F32)
    weight = tile[0:1, which * rows : (which + 1) * rows]
    numbers = [tile[1 + which : 2 + which, e * rows : (e + 1) * rows] for e in range(tile.shape[1] // rows)]
    return weight, numbers


def col_places(n, r):
    return [lax.rem((r ^ odd) + 2 * m, n) for m in range(n // 2) for odd in (0, 1)]


def row_places(n, r, c):
    return [lax.rem((c ^ 1 ^ odd) + 2 * (m + r), n) for odd in (0, 1) for m in range(n // 2)]


def picture_kernel(n, ab, rows, per, *refs):
    blocks, frames, out, image, slices = refs[:n], refs[n], refs[-3], refs[-2], refs[-1]
    r, c = lax.axis_index("row"), lax.axis_index("col")
    nf = frames.shape[0] // n
    for k in range(n):
        slices[c ^ k] = frames[k * nf : (k + 1) * nf, :].astype(F32)
    image[...] = jnp.zeros_like(image)
    for k in range(n):
        start = k * per // rows * rows
        shift = k * per - start
        wide = (per + shift + rows - 1) // rows * rows
        piece = slices[k]
        if shift:
            piece = pltpu.roll(piece, shift, 1)
        image[:, start : start + wide] += piece[:, :wide]
    parts = [image[:, b * rows : (b + 1) * rows] for b in range(ab)]
    for block, place in zip(blocks, row_places(n, r, c)):
        for which in range(2):
            weight, numbers = info(block, rows, which)
            chosen = []
            for number in numbers:
                pick = jnp.zeros((nf, rows), F32)
                for b in range(ab):
                    pick = jnp.where(number == float(b), parts[b], pick)
                chosen.append(pick)
            picked = jnp.concatenate(chosen, axis=1).astype(BF16)
            values = block[which * rows : (which + 1) * rows, :]
            result = lax.dot_general(picked, values, (((1,), (1,)), ((), ())), preferred_element_type=F32)
            out[2 * place + which] = (result * weight).astype(BF16)


def applied_kernel(n, rows, per, *refs):
    blocks, sums, out = refs[:n], refs[n : n + n // 2], refs[-1]
    r, c = lax.axis_index("row"), lax.axis_index("col")
    nf = out.shape[0]
    count = (per + rows - 1 + rows - 1) // rows
    first = c * per // rows
    wanted = [(first + k).astype(F32) for k in range(count)]
    totals = [jnp.zeros((nf, rows), F32) for _ in range(count)]
    for block, place in zip(blocks, row_places(n, r, c)):
        for which in range(2):
            _, numbers = info(block, rows, which)
            values = block[which * rows : (which + 1) * rows, :]
            result = sums[0][2 * place + which].astype(F32)
            for other in sums[1:]:
                result = result + other[2 * place + which].astype(F32)
            high = result.astype(BF16)
            low = (result - high.astype(F32)).astype(BF16)
            both = jnp.dot(jnp.concatenate([high, low], axis=0), values, preferred_element_type=F32)
            both = both[:nf] + both[nf:]
            for e, number in enumerate(numbers):
                part = both[:, e * rows : (e + 1) * rows]
                for k in range(count):
                    totals[k] = totals[k] + jnp.where(number == wanted[k], part, 0.0)
    image = jnp.concatenate(totals, axis=1)
    image = pltpu.roll(image, lax.rem(count * rows - (c * per - first * rows), count * rows), 1)
    out[...] = image[:, :per]


def dense_kernel(n, ab, rows, *refs):
    own_c, own_r, left, right = refs[:n], refs[n : 2 * n], refs[2 * n], refs[2 * n + 1]
    r, c = lax.axis_index("row"), lax.axis_index("col")
    eye = lax.broadcasted_iota(jnp.int32, (rows, rows), 0) == lax.broadcasted_iota(jnp.int32, (rows, rows), 1)
    for blocks, out, places, weighted in (
        (own_c, right, col_places(n, r), True),
        (own_r, left, row_places(n, r, c), False),
    ):
        for block, place in zip(blocks, places):
            base = place * (2 * rows)
            for which in range(2):
                weight, numbers = info(block, rows, which)
                values = block[which * rows : (which + 1) * rows, :]
                if weighted:
                    scale = jnp.where(eye, jnp.broadcast_to(weight, (rows, rows)), 0.0).astype(BF16)
                    values = jnp.dot(scale, values, preferred_element_type=F32)
                else:
                    values = values.astype(F32)
                at = pl.ds(pl.multiple_of(base + which * rows, rows), rows)
                for b in range(ab):
                    total = jnp.zeros((rows, rows), F32)
                    for e, number in enumerate(numbers):
                        total = jnp.where(number == float(b), values[:, e * rows : (e + 1) * rows], total)
                    out[at, b * rows : (b + 1) * rows] = total.astype(BF16)


def shards(n, slope_matrix, prior_matrix, slope_blocks, prior_blocks, weight_ids, valid_mask, noise_weights, prior_weights, frames):
    rows, width = slope_matrix.shape
    per, nf = frames.shape
    ab = per * n // rows
    packed, sent = pl.pallas_call(
        functools.partial(pack_kernel, ab),
        out_shape=(
            pltpu.VMEM((2 * rows + EXTRA, width), BF16),
            pltpu.VMEM((nf, width), BF16),
        ),
        in_specs=[VMEM, VMEM, SMEM, SMEM, VMEM, VMEM, VMEM, SMEM, VMEM],
        out_specs=(VMEM, VMEM),
        name="pack",
    )(
        slope_matrix,
        prior_matrix,
        slope_blocks,
        prior_blocks,
        weight_ids[None, :],
        valid_mask[None, :],
        prior_weights[None, :],
        noise_weights,
        frames.T,
    )
    half = n // 2
    firsts = [permute(packed, n, lambda r, c, m=m: (((c ^ 1) + 2 * (m + r)) % n, r)) for m in range(half)]
    row_side = firsts + [permute(firsts[m], n, lambda r, c: (r, c ^ 1)) for m in range(half)]
    col_side = [packed, permute(packed, n, lambda r, c: (r ^ 1, c))]
    for m in range(1, half):
        other = permute(packed, n, lambda r, c, m=m: ((r + 2 * m) % n, c))
        col_side += [other, permute(other, n, lambda r, c: (r ^ 1, c))]
    mine = sent
    for bit in range(n.bit_length() - 1):
        other = permute(mine, n, lambda r, c, bit=bit: (r, c ^ (1 << bit)))
        mine = jnp.concatenate([mine, other], axis=0)
    picture = pl.pallas_call(
        functools.partial(picture_kernel, n, ab, rows, per),
        out_shape=pltpu.VMEM((2 * n, nf, rows), BF16),
        in_specs=[VMEM] * (n + 1),
        out_specs=VMEM,
        scratch_shapes=[pltpu.VMEM((nf, ab * rows), F32), pltpu.VMEM((n, nf, width), F32)],
        compiler_params=SMALL,
        name="picture",
    )(*here(*row_side, mine))
    partner = permute(picture, n, lambda r, c: (r ^ 1, c))
    chip = (picture.astype(F32) + partner.astype(F32)).astype(BF16)
    sums = [chip] + [permute(chip, n, lambda r, c, m=m: ((r + 2 * m) % n, c)) for m in range(1, half)]
    applied = pl.pallas_call(
        functools.partial(applied_kernel, n, rows, per),
        out_shape=jax.ShapeDtypeStruct((nf, per), F32),
        in_specs=[VMEM] * (n + half),
        out_specs=VMEM,
        compiler_params=SMALL,
        name="applied",
    )(*here(*row_side, *sums))
    expand = pl.pallas_call(
        functools.partial(dense_kernel, n, ab, rows),
        out_shape=(pltpu.VMEM((2 * rows * n, ab * rows), BF16), pltpu.VMEM((2 * rows * n, ab * rows), BF16)),
        in_specs=[VMEM] * (2 * n),
        out_specs=(VMEM, VMEM),
        compiler_params=SMALL,
        name="dense",
    )
    left, right = expand(*here(*col_side, *row_side))
    gram = lax.dot_general(left, right, (((0,), (0,)), ((), ())), preferred_element_type=F32)
    return gram, applied.T


def solution(mesh):
    n = mesh.shape["row"]
    block = P(("groups", "row"), "col")
    line = P(("groups", "row"))
    whole = P(("groups", "row", "col"), None)
    in_specs = (block, block, block, block, line, line, P("groups"), line, whole)
    return jax.shard_map(
        functools.partial(shards, n), mesh=mesh, in_specs=in_specs, out_specs=(block, whole), check_vma=False
    )
```

profile of v0, /device:TPU:0, one launch (start us, length us, event | category | flops | bytes accessed | tf_op | source)
XLA Modules:
  0.0 30.9 jit_solution(16234388520287414945)
XLA Ops:
  0.6 1.1 %pack.1 = (bf16[272,256]{1,0:T(8,128)(2,1)S(1)}, bf16[64,256]{1,0:T(8,128)(2,1)S(1)}) custom-call(bf16[128,256]{1,0:T(8,128)(2,1)} %slope.1, bf16[128,256]{1,0:T(8,128)(2,1)} %prior.1, s32[1,2]{1,0:T(1,128)} %ids_s.1, s32[1,2]{1,0:T(1,128)} %ids_p.1, s32[1,64]{1,0:T(1,128)} %bitcast.9, s32[1,64]{1,0:T(1,128)} %bitcast.10, bf16[1,128]{1,0:T(2,128)(2,1)} %bitcast.11, ...), custom_call_target="tpu_custom_call" | custom-call | tf_op jit(solution)/shard_map/pack/pallas_call | solution.py:164
  1.7 3.1 %collective-permute-start.7 = (bf16[64,256]{1,0:T(8,128)(2,1)S(1)}, bf16[64,256]{1,0:T(8,128)(2,1)S(1)}, u32[]{:S(2)}, u32[]{:S(2)}) collective-permute-start(bf16[64,256]{1,0:T(8,128)(2,1)S(1)} %get-tuple-element.9), channel_id=1, source_target_pairs={{1,0},{0,1},{3,2},{2,3},{5,4},{4,5},{7,6},{6,7},{9,8},{8,9},{11,10... | collective-permute-start | bytes 98312 | tf_op jit(solution)/shard_map/ppermute | solution.py:29
  4.9 2.5 %collective-permute-start.4 = (bf16[272,256]{1,0:T(8,128)(2,1)S(1)}, bf16[272,256]{1,0:T(8,128)(2,1)S(1)}, u32[]{:S(2)}, u32[]{:S(2)}) collective-permute-start(bf16[272,256]{1,0:T(8,128)(2,1)S(1)} %get-tuple-element.6.refs_0_), channel_id=1, source_target_pairs={{12,0},{8,1},{4,2},{0,3},{5,4},{1,5},{13,6},{9,7},{14,8},{10,9},{6... | collective-permute-start | bytes 417800 | tf_op jit(solution)/shard_map/ppermute | solution.py:29
  7.3 0.0 collective-permute-start.3
  7.3 1.9 %collective-permute-start.1 = (bf16[272,256]{1,0:T(8,128)(2,1)S(1)}, bf16[272,256]{1,0:T(8,128)(2,1)S(1)}, u32[]{:S(2)}, u32[]{:S(2)}) collective-permute-start(bf16[272,256]{1,0:T(8,128)(2,1)S(1)} %get-tuple-element.6.refs_0_), channel_id=1, source_target_pairs={{8,0},{9,1},{10,2},{11,3},{12,4},{13,5},{14,6},{15,7},{0,8},{1,9},... | collective-permute-start | bytes 417800 | tf_op jit(solution)/shard_map/ppermute | solution.py:29
  9.2 0.0 collective-permute-done.7
  9.2 0.6 %collective-permute-start.8 = (bf16[128,256]{1,0:T(8,128)(2,1)S(1)}, bf16[128,256]{1,0:T(8,128)(2,1)S(1)}, u32[]{:S(2)}, u32[]{:S(2)}) collective-permute-start(bf16[128,256]{1,0:T(8,128)(2,1)S(1)} %pad_maximum_fusion.1), channel_id=1, source_target_pairs={{2,0},{3,1},{0,2},{1,3},{6,4},{7,5},{4,6},{5,7},{10,8},{11,9},{8,1... | collective-permute-start | bytes 196616 | tf_op jit(solution)/shard_map/ppermute | solution.py:29
  9.8 1.6 %collective-permute-done.4.refs_5_.refs_1_ = bf16[272,256]{1,0:T(8,128)(2,1)S(1)} collective-permute-done((bf16[272,256]{1,0:T(8,128)(2,1)S(1)}, bf16[272,256]{1,0:T(8,128)(2,1)S(1)}, u32[]{:S(2)}, u32[]{:S(2)}) %collective-permute-start.4) | collective-permute-done | bytes 139296 | tf_op jit(solution)/shard_map/ppermute | solution.py:29
  11.4 0.0 collective-permute-start.6
  11.4 3.0 %collective-permute-done.3.refs_4_.refs_0_ = bf16[272,256]{1,0:T(8,128)(2,1)S(1)} collective-permute-done((bf16[272,256]{1,0:T(8,128)(2,1)S(1)}, bf16[272,256]{1,0:T(8,128)(2,1)S(1)}, u32[]{:S(2)}, u32[]{:S(2)}) %collective-permute-start.3) | collective-permute-done | bytes 139296 | tf_op jit(solution)/shard_map/ppermute | solution.py:29
  14.4 2.5 %collective-permute-start.5 = (bf16[272,256]{1,0:T(8,128)(2,1)S(1)}, bf16[272,256]{1,0:T(8,128)(2,1)S(1)}, u32[]{:S(2)}, u32[]{:S(2)}) collective-permute-start(bf16[272,256]{1,0:T(8,128)(2,1)S(1)} %collective-permute-done.3.refs_4_.refs_0_), channel_id=1, source_target_pairs={{1,0},{0,1},{3,2},{2,3},{5,4},{4,5},{7,6},{6,7},{9,8},{8,9},{11,10... | collective-permute-start | bytes 417800 | tf_op jit(solution)/shard_map/ppermute | solution.py:29
  16.8 0.0 collective-permute-start
  16.8 0.0 collective-permute-done.1.refs_2_
  16.8 0.5 %collective-permute-start.2 = (bf16[272,256]{1,0:T(8,128)(2,1)S(1)}, bf16[272,256]{1,0:T(8,128)(2,1)S(1)}, u32[]{:S(2)}, u32[]{:S(2)}) collective-permute-start(bf16[272,256]{1,0:T(8,128)(2,1)S(1)} %collective-permute-done.1.refs_2_), channel_id=1, source_target_pairs={{4,0},{5,1},{6,2},{7,3},{0,4},{1,5},{2,6},{3,7},{12,8},{13,9},{14,... | collective-permute-start | bytes 417800 | tf_op jit(solution)/shard_map/ppermute | solution.py:29
  17.3 0.8 %collective-permute-done.8 = bf16[128,256]{1,0:T(8,128)(2,1)S(1)} collective-permute-done((bf16[128,256]{1,0:T(8,128)(2,1)S(1)}, bf16[128,256]{1,0:T(8,128)(2,1)S(1)}, u32[]{:S(2)}, u32[]{:S(2)}) %collective-permute-start.8) | collective-permute-done | bytes 65568 | tf_op jit(solution)/shard_map/ppermute | solution.py:29
  18.2 0.9 %collective-permute-done.6.refs_7_.refs_3_ = bf16[272,256]{1,0:T(8,128)(2,1)S(1)} collective-permute-done((bf16[272,256]{1,0:T(8,128)(2,1)S(1)}, bf16[272,256]{1,0:T(8,128)(2,1)S(1)}, u32[]{:S(2)}, u32[]{:S(2)}) %collective-permute-start.6) | collective-permute-done | bytes 139296 | tf_op jit(solution)/shard_map/ppermute | solution.py:29
  19.1 2.5 %collective-permute-done.5.refs_6_.refs_2_ = bf16[272,256]{1,0:T(8,128)(2,1)S(1)} collective-permute-done((bf16[272,256]{1,0:T(8,128)(2,1)S(1)}, bf16[272,256]{1,0:T(8,128)(2,1)S(1)}, u32[]{:S(2)}, u32[]{:S(2)}) %collective-permute-start.5) | collective-permute-done | bytes 139296 | tf_op jit(solution)/shard_map/ppermute | solution.py:29
  21.6 0.4 %picture.1 = bf16[8,64,128]{2,1,0:T(8,128)(2,1)S(1)} custom-call(bf16[272,256]{1,0:T(8,128)(2,1)S(1)} %collective-permute-done.3.refs_4_.refs_0_, bf16[272,256]{1,0:T(8,128)(2,1)S(1)} %collective-permute-done.4.refs_5_.refs_1_, bf16[272,256]{1,0:T(8,128)(2,1)S(1)} %collective-permute-done.5.refs_6_.refs_2_, ...), custom_call_target="tpu_custom_call" | custom-call | tf_op jit(solution)/shard_map/picture/pallas_call | solution.py:195
  22.0 0.1 collective-permute-start.9
  22.1 0.0 collective-permute-done.refs_1_
  22.1 0.0 collective-permute-done.2.refs_3_
  22.1 1.0 %dense.1 = (bf16[1024,768]{1,0:T(8,128)(2,1)S(1)}, bf16[1024,768]{1,0:T(8,128)(2,1)S(1)}) custom-call(bf16[272,256]{1,0:T(8,128)(2,1)S(1)} %get-tuple-element.6.refs_0_, bf16[272,256]{1,0:T(8,128)(2,1)S(1)} %collective-permute-done.refs_1_, bf16[272,256]{1,0:T(8,128)(2,1)S(1)} %collective-permute-done.1.refs_2_, ...), custom_call_target="tpu_custom_call" | custom-call | tf_op jit(solution)/shard_map/dense/pallas_call | solution.py:223
  23.2 0.3 collective-permute-done.9
  23.5 2.5 %collective-permute-start.10 = (bf16[8,64,128]{2,1,0:T(8,128)(2,1)S(1)}, bf16[8,64,128]{2,1,0:T(8,128)(2,1)S(1)}, u32[]{:S(2)}, u32[]{:S(2)}) collective-permute-start(bf16[8,64,128]{2,1,0:T(8,128)(2,1)S(1)} %add_convert_fusion.refs_4_), channel_id=1, source_target_pairs={{8,0},{9,1},{10,2},{11,3},{12,4},{13,5},{14,6},{15,7},{0,8},{1,9},... | collective-permute-start | bytes 393224 | tf_op jit(solution)/shard_map/ppermute | solution.py:29
  26.0 2.8 %fusion = f32[768,768]{1,0:T(8,128)} fusion(bf16[1024,768]{1,0:T(8,128)(2,1)S(1)} %get-tuple-element.7, bf16[1024,768]{1,0:T(8,128)(2,1)S(1)} %get-tuple-element.8), kind=kOutput, calls=%fused_computation.3 | convolution fusion | flops 1207959552 | bytes 5505024 | tf_op jit(solution)/shard_map/dot_general | solution.py:224
  28.9 1.0 %collective-permute-done.10.refs_5_ = bf16[8,64,128]{2,1,0:T(8,128)(2,1)S(1)} collective-permute-done((bf16[8,64,128]{2,1,0:T(8,128)(2,1)S(1)}, bf16[8,64,128]{2,1,0:T(8,128)(2,1)S(1)}, u32[]{:S(2)}, u32[]{:S(2)}) %collective-permute-start.10) | collective-permute-done | bytes 131104 | tf_op jit(solution)/shard_map/ppermute | solution.py:29
  29.9 1.0 %applied.1 = f32[64,192]{1,0:T(8,128)} custom-call(bf16[272,256]{1,0:T(8,128)(2,1)S(1)} %collective-permute-done.3.refs_4_.refs_0_, bf16[272,256]{1,0:T(8,128)(2,1)S(1)} %collective-permute-done.4.refs_5_.refs_1_, bf16[272,256]{1,0:T(8,128)(2,1)S(1)} %collective-permute-done.5.refs_6_.refs_2_, bf16[272,256]{1,0:T(8,128)(2,1)S(1)} %collective-permute-done.6.refs_7_.refs_3_, ...), custom_call_target="tpu_custom_call" | custom-call | tf_op jit(solution)/shard_map/applied/pallas_call | solution.py:207
  (3 shorter events, 0.1 us)
Async XLA Ops:
  1.7 7.5 %collective-permute-start.7 = (bf16[64,256]{1,0:T(8,128)(2,1)S(1)}, bf16[64,256]{1,0:T(8,128)(2,1)S(1)}, u32[]{:S(2)}, u32[]{:S(2)}) collective-permute-start(bf16[64,256]{1,0:T(8,128)(2,1)S(1)} %get-tuple-element.9), channel_id=1, source_target_pairs={{1,0},{0,1},{3,2},{2,3},{5,4},{4,5},{7,6},{6,7},{9,8},{8,9},{11,10... | collective-permute-start | bytes 98312 | tf_op jit(solution)/shard_map/ppermute | solution.py:29
  4.9 6.5 %collective-permute-start.4 = (bf16[272,256]{1,0:T(8,128)(2,1)S(1)}, bf16[272,256]{1,0:T(8,128)(2,1)S(1)}, u32[]{:S(2)}, u32[]{:S(2)}) collective-permute-start(bf16[272,256]{1,0:T(8,128)(2,1)S(1)} %get-tuple-element.6.refs_0_), channel_id=1, source_target_pairs={{12,0},{8,1},{4,2},{0,3},{5,4},{1,5},{13,6},{9,7},{14,8},{10,9},{6... | collective-permute-start | bytes 417800 | tf_op jit(solution)/shard_map/ppermute | solution.py:29
  7.3 7.0 %collective-permute-start.3 = (bf16[272,256]{1,0:T(8,128)(2,1)S(1)}, bf16[272,256]{1,0:T(8,128)(2,1)S(1)}, u32[]{:S(2)}, u32[]{:S(2)}) collective-permute-start(bf16[272,256]{1,0:T(8,128)(2,1)S(1)} %get-tuple-element.6.refs_0_), channel_id=1, source_target_pairs={{4,0},{0,1},{12,2},{8,3},{13,4},{9,5},{5,6},{1,7},{6,8},{2,9},{14,... | collective-permute-start | bytes 417800 | tf_op jit(solution)/shard_map/ppermute | solution.py:29
  7.3 9.5 %collective-permute-start.1 = (bf16[272,256]{1,0:T(8,128)(2,1)S(1)}, bf16[272,256]{1,0:T(8,128)(2,1)S(1)}, u32[]{:S(2)}, u32[]{:S(2)}) collective-permute-start(bf16[272,256]{1,0:T(8,128)(2,1)S(1)} %get-tuple-element.6.refs_0_), channel_id=1, source_target_pairs={{8,0},{9,1},{10,2},{11,3},{12,4},{13,5},{14,6},{15,7},{0,8},{1,9},... | collective-permute-start | bytes 417800 | tf_op jit(solution)/shard_map/ppermute | solution.py:29
  9.2 8.9 %collective-permute-start.8 = (bf16[128,256]{1,0:T(8,128)(2,1)S(1)}, bf16[128,256]{1,0:T(8,128)(2,1)S(1)}, u32[]{:S(2)}, u32[]{:S(2)}) collective-permute-start(bf16[128,256]{1,0:T(8,128)(2,1)S(1)} %pad_maximum_fusion.1), channel_id=1, source_target_pairs={{2,0},{3,1},{0,2},{1,3},{6,4},{7,5},{4,6},{5,7},{10,8},{11,9},{8,1... | collective-permute-start | bytes 196616 | tf_op jit(solution)/shard_map/ppermute | solution.py:29
  11.4 7.7 %collective-permute-start.6 = (bf16[272,256]{1,0:T(8,128)(2,1)S(1)}, bf16[272,256]{1,0:T(8,128)(2,1)S(1)}, u32[]{:S(2)}, u32[]{:S(2)}) collective-permute-start(bf16[272,256]{1,0:T(8,128)(2,1)S(1)} %collective-permute-done.4.refs_5_.refs_1_), channel_id=1, source_target_pairs={{1,0},{0,1},{3,2},{2,3},{5,4},{4,5},{7,6},{6,7},{9,8},{8,9},{11,10... | collective-permute-start | bytes 417800 | tf_op jit(solution)/shard_map/ppermute | solution.py:29
  14.4 7.3 %collective-permute-start.5 = (bf16[272,256]{1,0:T(8,128)(2,1)S(1)}, bf16[272,256]{1,0:T(8,128)(2,1)S(1)}, u32[]{:S(2)}, u32[]{:S(2)}) collective-permute-start(bf16[272,256]{1,0:T(8,128)(2,1)S(1)} %collective-permute-done.3.refs_4_.refs_0_), channel_id=1, source_target_pairs={{1,0},{0,1},{3,2},{2,3},{5,4},{4,5},{7,6},{6,7},{9,8},{8,9},{11,10... | collective-permute-start | bytes 417800 | tf_op jit(solution)/shard_map/ppermute | solution.py:29
  16.8 5.3 %collective-permute-start = (bf16[272,256]{1,0:T(8,128)(2,1)S(1)}, bf16[272,256]{1,0:T(8,128)(2,1)S(1)}, u32[]{:S(2)}, u32[]{:S(2)}) collective-permute-start(bf16[272,256]{1,0:T(8,128)(2,1)S(1)} %get-tuple-element.6.refs_0_), channel_id=1, source_target_pairs={{4,0},{5,1},{6,2},{7,3},{0,4},{1,5},{2,6},{3,7},{12,8},{13,9},{14,... | collective-permute-start | bytes 417800 | tf_op jit(solution)/shard_map/ppermute | solution.py:29
  16.8 5.3 %collective-permute-start.2 = (bf16[272,256]{1,0:T(8,128)(2,1)S(1)}, bf16[272,256]{1,0:T(8,128)(2,1)S(1)}, u32[]{:S(2)}, u32[]{:S(2)}) collective-permute-start(bf16[272,256]{1,0:T(8,128)(2,1)S(1)} %collective-permute-done.1.refs_2_), channel_id=1, source_target_pairs={{4,0},{5,1},{6,2},{7,3},{0,4},{1,5},{2,6},{3,7},{12,8},{13,9},{14,... | collective-permute-start | bytes 417800 | tf_op jit(solution)/shard_map/ppermute | solution.py:29
  22.0 1.4 %collective-permute-start.9 = (bf16[8,64,128]{2,1,0:T(8,128)(2,1)S(1)}, bf16[8,64,128]{2,1,0:T(8,128)(2,1)S(1)}, u32[]{:S(2)}, u32[]{:S(2)}) collective-permute-start(bf16[8,64,128]{2,1,0:T(8,128)(2,1)S(1)} %picture.1), channel_id=1, source_target_pairs={{4,0},{5,1},{6,2},{7,3},{0,4},{1,5},{2,6},{3,7},{12,8},{13,9},{14,... | collective-permute-start | bytes 393224 | tf_op jit(solution)/shard_map/ppermute | solution.py:29
  23.5 6.4 %collective-permute-start.10 = (bf16[8,64,128]{2,1,0:T(8,128)(2,1)S(1)}, bf16[8,64,128]{2,1,0:T(8,128)(2,1)S(1)}, u32[]{:S(2)}, u32[]{:S(2)}) collective-permute-start(bf16[8,64,128]{2,1,0:T(8,128)(2,1)S(1)} %add_convert_fusion.refs_4_), channel_id=1, source_target_pairs={{8,0},{9,1},{10,2},{11,3},{12,4},{13,5},{14,6},{15,7},{0,8},{1,9},... | collective-permute-start | bytes 393224 | tf_op jit(solution)/shard_map/ppermute | solution.py:29
where the time goes:
time: 31.1 us; the launch traced here: 30.9 us
  starting transfers between devices  13.6 us (44%)
  waiting for transfers between devices  10.1 us (32%)
  Pallas kernels  3.56 us (11%)
  matrix products  2.85 us (9%)
  between operations  0.69 us (2%)
    ppermute x11, starting transfers between devices, permute(): return lax.ppermute(value, ('row', 'col'), pairs)  13.6 us
    ppermute x11, waiting for transfers between devices, permute(): return lax.ppermute(value, ('row', 'col'), pairs)  10.1 us
    dot_general x1, matrix products, shards(): lax.dot_general(left, right, (((0,), (0,)), ((), ())), preferred_element_...  2.85 us
    pallas_call x1, Pallas kernels, shards(): pl.pallas_call(functools.partial(pack_kernel, ab), out_shape=(pltpu.VMEM(...  1.11 us
    pallas_call x1, Pallas kernels, shards(): left, right = expand(*here(*col_side, *row_side))  1.02 us
    pallas_call x1, Pallas kernels, shards(): pl.pallas_call(functools.partial(applied_kernel, n, rows, per), out_shape...  1.02 us
  transfers between devices with their start and end apart: 11, of which 7 were waited for; matrix products, arithmetic and copies ran while one was open for 9% of the time, Pallas kernels for 5%

commit v1 on v0

--- a/solution.py
+++ b/solution.py
@@ -65,11 +65,11 @@
 
 
 def col_places(n, r):
-    return [lax.rem((r ^ odd) + 2 * m, n) for m in range(n // 2) for odd in (0, 1)]
+    return [lax.rem((r ^ odd ^ min(m, 1)) + 2 * m, n) for m in range(n // 2) for odd in (0, 1)]
 
 
 def row_places(n, r, c):
-    return [lax.rem((c ^ 1 ^ odd) + 2 * (m + r), n) for odd in (0, 1) for m in range(n // 2)]
+    return [lax.rem((c ^ odd ^ 1) + 2 * (m + r), n) for odd in (0, 1) for m in range(n // 2)]
 
 
 def picture_kernel(n, ab, rows, per, *refs):
@@ -186,7 +186,7 @@
     row_side = firsts + [permute(firsts[m], n, lambda r, c: (r, c ^ 1)) for m in range(half)]
     col_side = [packed, permute(packed, n, lambda r, c: (r ^ 1, c))]
     for m in range(1, half):
-        other = permute(packed, n, lambda r, c, m=m: ((r + 2 * m) % n, c))
+        other = permute(packed, n, lambda r, c, m=m: (((r ^ 1) + 2 * m) % n, c))
         col_side += [other, permute(other, n, lambda r, c: (r ^ 1, c))]
     mine = sent
     for bit in range(n.bit_length() - 1):
@@ -203,7 +203,7 @@
     )(*here(*row_side, mine))
     partner = permute(picture, n, lambda r, c: (r ^ 1, c))
     chip = (picture.astype(F32) + partner.astype(F32)).astype(BF16)
-    sums = [chip] + [permute(chip, n, lambda r, c, m=m: ((r + 2 * m) % n, c)) for m in range(1, half)]
+    sums = [chip] + [permute(chip, n, lambda r, c, m=m: (((r ^ 1) + 2 * m) % n, c)) for m in range(1, half)]
     applied = pl.pallas_call(
         functools.partial(applied_kernel, n, rows, per),
         out_shape=jax.ShapeDtypeStruct((nf, per), F32),

time: 31.1 us -> 30.5 us (0.981)
  waiting for transfers between devices: 10.1 us -> 9.48 us
    ppermute x11, waiting for transfers between devices: 10.1 us -> 9.48 us  [permute(): return lax.ppermute(value, ('row', 'col'), pairs)]
where the time goes in v1:
time: 30.5 us; the launch traced here: 30.3 us
  starting transfers between devices  13.7 us (45%)
  waiting for transfers between devices  9.48 us (31%)
  Pallas kernels  3.56 us (12%)
  matrix products  2.84 us (9%)
  between operations  0.7 us (2%)
    ppermute x11, starting transfers between devices, permute(): return lax.ppermute(value, ('row', 'col'), pairs)  13.7 us
    ppermute x11, waiting for transfers between devices, permute(): return lax.ppermute(value, ('row', 'col'), pairs)  9.48 us
    dot_general x1, matrix products, shards(): lax.dot_general(left, right, (((0,), (0,)), ((), ())), preferred_element_...  2.84 us
    pallas_call x1, Pallas kernels, shards(): pl.pallas_call(functools.partial(pack_kernel, ab), out_shape=(pltpu.VMEM(...  1.11 us
    pallas_call x1, Pallas kernels, shards(): pl.pallas_call(functools.partial(applied_kernel, n, rows, per), out_shape...  1.02 us
    pallas_call x1, Pallas kernels, shards(): left, right = expand(*here(*col_side, *row_side))  1.02 us
  transfers between devices with their start and end apart: 11, of which 7 were waited for; matrix products, arithmetic and copies ran while one was open for 9% of the time, Pallas kernels for 5%

profile of v1, /device:TPU:0, one launch (start us, length us, event | category | flops | bytes accessed | tf_op | source)
XLA Modules:
  0.0 30.3 jit_solution(12471191621457657110)
XLA Ops:
  0.6 1.1 %pack.1 = (bf16[272,256]{1,0:T(8,128)(2,1)S(1)}, bf16[64,256]{1,0:T(8,128)(2,1)S(1)}) custom-call(bf16[128,256]{1,0:T(8,128)(2,1)} %slope.1, bf16[128,256]{1,0:T(8,128)(2,1)} %prior.1, s32[1,2]{1,0:T(1,128)} %ids_s.1, s32[1,2]{1,0:T(1,128)} %ids_p.1, s32[1,64]{1,0:T(1,128)} %bitcast.9, s32[1,64]{1,0:T(1,128)} %bitcast.10, bf16[1,128]{1,0:T(2,128)(2,1)} %bitcast.11, ...), custom_call_target="tpu_custom_call" | custom-call | tf_op jit(solution)/shard_map/pack/pallas_call | solution.py:164
  1.7 3.1 %collective-permute-start.7 = (bf16[64,256]{1,0:T(8,128)(2,1)S(1)}, bf16[64,256]{1,0:T(8,128)(2,1)S(1)}, u32[]{:S(2)}, u32[]{:S(2)}) collective-permute-start(bf16[64,256]{1,0:T(8,128)(2,1)S(1)} %get-tuple-element.9), channel_id=1, source_target_pairs={{1,0},{0,1},{3,2},{2,3},{5,4},{4,5},{7,6},{6,7},{9,8},{8,9},{11,10... | collective-permute-start | bytes 98312 | tf_op jit(solution)/shard_map/ppermute | solution.py:29
  4.9 2.5 %collective-permute-start.4 = (bf16[272,256]{1,0:T(8,128)(2,1)S(1)}, bf16[272,256]{1,0:T(8,128)(2,1)S(1)}, u32[]{:S(2)}, u32[]{:S(2)}) collective-permute-start(bf16[272,256]{1,0:T(8,128)(2,1)S(1)} %get-tuple-element.6.refs_0_), channel_id=1, source_target_pairs={{12,0},{8,1},{4,2},{0,3},{5,4},{1,5},{13,6},{9,7},{14,8},{10,9},{6... | collective-permute-start | bytes 417800 | tf_op jit(solution)/shard_map/ppermute | solution.py:29
  7.3 0.0 collective-permute-start.3
  7.3 2.7 %collective-permute-start.1 = (bf16[272,256]{1,0:T(8,128)(2,1)S(1)}, bf16[272,256]{1,0:T(8,128)(2,1)S(1)}, u32[]{:S(2)}, u32[]{:S(2)}) collective-permute-start(bf16[272,256]{1,0:T(8,128)(2,1)S(1)} %get-tuple-element.6.refs_0_), channel_id=1, source_target_pairs={{12,0},{13,1},{14,2},{15,3},{8,4},{9,5},{10,6},{11,7},{4,8},{5,9},... | collective-permute-start | bytes 417800 | tf_op jit(solution)/shard_map/ppermute | solution.py:29
  10.0 0.0 collective-permute-done.7
  10.0 0.1 collective-permute-start.8
  10.1 1.3 %collective-permute-done.4.refs_5_.refs_1_ = bf16[272,256]{1,0:T(8,128)(2,1)S(1)} collective-permute-done((bf16[272,256]{1,0:T(8,128)(2,1)S(1)}, bf16[272,256]{1,0:T(8,128)(2,1)S(1)}, u32[]{:S(2)}, u32[]{:S(2)}) %collective-permute-start.4) | collective-permute-done | bytes 139296 | tf_op jit(solution)/shard_map/ppermute | solution.py:29
  11.4 0.0 collective-permute-start.6
  11.4 3.0 %collective-permute-done.3.refs_4_.refs_0_ = bf16[272,256]{1,0:T(8,128)(2,1)S(1)} collective-permute-done((bf16[272,256]{1,0:T(8,128)(2,1)S(1)}, bf16[272,256]{1,0:T(8,128)(2,1)S(1)}, u32[]{:S(2)}, u32[]{:S(2)}) %collective-permute-start.3) | collective-permute-done | bytes 139296 | tf_op jit(solution)/shard_map/ppermute | solution.py:29
  14.4 2.5 %collective-permute-start.5 = (bf16[272,256]{1,0:T(8,128)(2,1)S(1)}, bf16[272,256]{1,0:T(8,128)(2,1)S(1)}, u32[]{:S(2)}, u32[]{:S(2)}) collective-permute-start(bf16[272,256]{1,0:T(8,128)(2,1)S(1)} %collective-permute-done.3.refs_4_.refs_0_), channel_id=1, source_target_pairs={{1,0},{0,1},{3,2},{2,3},{5,4},{4,5},{7,6},{6,7},{9,8},{8,9},{11,10... | collective-permute-start | bytes 417800 | tf_op jit(solution)/shard_map/ppermute | solution.py:29
  16.9 0.0 collective-permute-start
  16.9 0.0 collective-permute-done.1.refs_2_
  16.9 0.5 %collective-permute-start.2 = (bf16[272,256]{1,0:T(8,128)(2,1)S(1)}, bf16[272,256]{1,0:T(8,128)(2,1)S(1)}, u32[]{:S(2)}, u32[]{:S(2)}) collective-permute-start(bf16[272,256]{1,0:T(8,128)(2,1)S(1)} %collective-permute-done.1.refs_2_), channel_id=1, source_target_pairs={{4,0},{5,1},{6,2},{7,3},{0,4},{1,5},{2,6},{3,7},{12,8},{13,9},{14,... | collective-permute-start | bytes 417800 | tf_op jit(solution)/shard_map/ppermute | solution.py:29
  17.4 0.8 %collective-permute-done.8 = bf16[128,256]{1,0:T(8,128)(2,1)S(1)} collective-permute-done((bf16[128,256]{1,0:T(8,128)(2,1)S(1)}, bf16[128,256]{1,0:T(8,128)(2,1)S(1)}, u32[]{:S(2)}, u32[]{:S(2)}) %collective-permute-start.8) | collective-permute-done | bytes 65568 | tf_op jit(solution)/shard_map/ppermute | solution.py:29
  18.2 0.8 %collective-permute-done.6.refs_7_.refs_3_ = bf16[272,256]{1,0:T(8,128)(2,1)S(1)} collective-permute-done((bf16[272,256]{1,0:T(8,128)(2,1)S(1)}, bf16[272,256]{1,0:T(8,128)(2,1)S(1)}, u32[]{:S(2)}, u32[]{:S(2)}) %collective-permute-start.6) | collective-permute-done | bytes 139296 | tf_op jit(solution)/shard_map/ppermute | solution.py:29
  19.0 2.6 %collective-permute-done.5.refs_6_.refs_2_ = bf16[272,256]{1,0:T(8,128)(2,1)S(1)} collective-permute-done((bf16[272,256]{1,0:T(8,128)(2,1)S(1)}, bf16[272,256]{1,0:T(8,128)(2,1)S(1)}, u32[]{:S(2)}, u32[]{:S(2)}) %collective-permute-start.5) | collective-permute-done | bytes 139296 | tf_op jit(solution)/shard_map/ppermute | solution.py:29
  21.6 0.4 %picture.1 = bf16[8,64,128]{2,1,0:T(8,128)(2,1)S(1)} custom-call(bf16[272,256]{1,0:T(8,128)(2,1)S(1)} %collective-permute-done.3.refs_4_.refs_0_, bf16[272,256]{1,0:T(8,128)(2,1)S(1)} %collective-permute-done.4.refs_5_.refs_1_, bf16[272,256]{1,0:T(8,128)(2,1)S(1)} %collective-permute-done.5.refs_6_.refs_2_, ...), custom_call_target="tpu_custom_call" | custom-call | tf_op jit(solution)/shard_map/picture/pallas_call | solution.py:195
  22.0 0.1 collective-permute-start.9
  22.1 0.0 collective-permute-done.refs_1_
  22.1 0.0 collective-permute-done.2.refs_3_
  22.1 1.0 %dense.1 = (bf16[1024,768]{1,0:T(8,128)(2,1)S(1)}, bf16[1024,768]{1,0:T(8,128)(2,1)S(1)}) custom-call(bf16[272,256]{1,0:T(8,128)(2,1)S(1)} %get-tuple-element.6.refs_0_, bf16[272,256]{1,0:T(8,128)(2,1)S(1)} %collective-permute-done.refs_1_, bf16[272,256]{1,0:T(8,128)(2,1)S(1)} %collective-permute-done.1.refs_2_, ...), custom_call_target="tpu_custom_call" | custom-call | tf_op jit(solution)/shard_map/dense/pallas_call | solution.py:223
  23.1 0.3 collective-permute-done.9
  23.4 2.3 %collective-permute-start.10 = (bf16[8,64,128]{2,1,0:T(8,128)(2,1)S(1)}, bf16[8,64,128]{2,1,0:T(8,128)(2,1)S(1)}, u32[]{:S(2)}, u32[]{:S(2)}) collective-permute-start(bf16[8,64,128]{2,1,0:T(8,128)(2,1)S(1)} %add_convert_fusion.refs_4_), channel_id=1, source_target_pairs={{12,0},{13,1},{14,2},{15,3},{8,4},{9,5},{10,6},{11,7},{4,8},{5,9},... | collective-permute-start | bytes 393224 | tf_op jit(solution)/shard_map/ppermute | solution.py:29
  25.7 2.8 %fusion = f32[768,768]{1,0:T(8,128)} fusion(bf16[1024,768]{1,0:T(8,128)(2,1)S(1)} %get-tuple-element.7, bf16[1024,768]{1,0:T(8,128)(2,1)S(1)} %get-tuple-element.8), kind=kOutput, calls=%fused_computation.3 | convolution fusion | flops 1207959552 | bytes 5505024 | tf_op jit(solution)/shard_map/dot_general | solution.py:224
  28.6 0.7 %collective-permute-done.10.refs_5_ = bf16[8,64,128]{2,1,0:T(8,128)(2,1)S(1)} collective-permute-done((bf16[8,64,128]{2,1,0:T(8,128)(2,1)S(1)}, bf16[8,64,128]{2,1,0:T(8,128)(2,1)S(1)}, u32[]{:S(2)}, u32[]{:S(2)}) %collective-permute-start.10) | collective-permute-done | bytes 131104 | tf_op jit(solution)/shard_map/ppermute | solution.py:29
  29.3 1.0 %applied.1 = f32[64,192]{1,0:T(8,128)} custom-call(bf16[272,256]{1,0:T(8,128)(2,1)S(1)} %collective-permute-done.3.refs_4_.refs_0_, bf16[272,256]{1,0:T(8,128)(2,1)S(1)} %collective-permute-done.4.refs_5_.refs_1_, bf16[272,256]{1,0:T(8,128)(2,1)S(1)} %collective-permute-done.5.refs_6_.refs_2_, bf16[272,256]{1,0:T(8,128)(2,1)S(1)} %collective-permute-done.6.refs_7_.refs_3_, ...), custom_call_target="tpu_custom_call" | custom-call | tf_op jit(solution)/shard_map/applied/pallas_call | solution.py:207
  (3 shorter events, 0.1 us)
Async XLA Ops:
  1.7 8.3 %collective-permute-start.7 = (bf16[64,256]{1,0:T(8,128)(2,1)S(1)}, bf16[64,256]{1,0:T(8,128)(2,1)S(1)}, u32[]{:S(2)}, u32[]{:S(2)}) collective-permute-start(bf16[64,256]{1,0:T(8,128)(2,1)S(1)} %get-tuple-element.9), channel_id=1, source_target_pairs={{1,0},{0,1},{3,2},{2,3},{5,4},{4,5},{7,6},{6,7},{9,8},{8,9},{11,10... | collective-permute-start | bytes 98312 | tf_op jit(solution)/shard_map/ppermute | solution.py:29
  4.9 6.6 %collective-permute-start.4 = (bf16[272,256]{1,0:T(8,128)(2,1)S(1)}, bf16[272,256]{1,0:T(8,128)(2,1)S(1)}, u32[]{:S(2)}, u32[]{:S(2)}) collective-permute-start(bf16[272,256]{1,0:T(8,128)(2,1)S(1)} %get-tuple-element.6.refs_0_), channel_id=1, source_target_pairs={{12,0},{8,1},{4,2},{0,3},{5,4},{1,5},{13,6},{9,7},{14,8},{10,9},{6... | collective-permute-start | bytes 417800 | tf_op jit(solution)/shard_map/ppermute | solution.py:29
  7.3 7.1 %collective-permute-start.3 = (bf16[272,256]{1,0:T(8,128)(2,1)S(1)}, bf16[272,256]{1,0:T(8,128)(2,1)S(1)}, u32[]{:S(2)}, u32[]{:S(2)}) collective-permute-start(bf16[272,256]{1,0:T(8,128)(2,1)S(1)} %get-tuple-element.6.refs_0_), channel_id=1, source_target_pairs={{4,0},{0,1},{12,2},{8,3},{13,4},{9,5},{5,6},{1,7},{6,8},{2,9},{14,... | collective-permute-start | bytes 417800 | tf_op jit(solution)/shard_map/ppermute | solution.py:29
  7.3 9.6 %collective-permute-start.1 = (bf16[272,256]{1,0:T(8,128)(2,1)S(1)}, bf16[272,256]{1,0:T(8,128)(2,1)S(1)}, u32[]{:S(2)}, u32[]{:S(2)}) collective-permute-start(bf16[272,256]{1,0:T(8,128)(2,1)S(1)} %get-tuple-element.6.refs_0_), channel_id=1, source_target_pairs={{12,0},{13,1},{14,2},{15,3},{8,4},{9,5},{10,6},{11,7},{4,8},{5,9},... | collective-permute-start | bytes 417800 | tf_op jit(solution)/shard_map/ppermute | solution.py:29
  10.0 8.2 %collective-permute-start.8 = (bf16[128,256]{1,0:T(8,128)(2,1)S(1)}, bf16[128,256]{1,0:T(8,128)(2,1)S(1)}, u32[]{:S(2)}, u32[]{:S(2)}) collective-permute-start(bf16[128,256]{1,0:T(8,128)(2,1)S(1)} %pad_maximum_fusion.1), channel_id=1, source_target_pairs={{2,0},{3,1},{0,2},{1,3},{6,4},{7,5},{4,6},{5,7},{10,8},{11,9},{8,1... | collective-permute-start | bytes 196616 | tf_op jit(solution)/shard_map/ppermute | solution.py:29
  11.4 7.6 %collective-permute-start.6 = (bf16[272,256]{1,0:T(8,128)(2,1)S(1)}, bf16[272,256]{1,0:T(8,128)(2,1)S(1)}, u32[]{:S(2)}, u32[]{:S(2)}) collective-permute-start(bf16[272,256]{1,0:T(8,128)(2,1)S(1)} %collective-permute-done.4.refs_5_.refs_1_), channel_id=1, source_target_pairs={{1,0},{0,1},{3,2},{2,3},{5,4},{4,5},{7,6},{6,7},{9,8},{8,9},{11,10... | collective-permute-start | bytes 417800 | tf_op jit(solution)/shard_map/ppermute | solution.py:29
  14.4 7.1 %collective-permute-start.5 = (bf16[272,256]{1,0:T(8,128)(2,1)S(1)}, bf16[272,256]{1,0:T(8,128)(2,1)S(1)}, u32[]{:S(2)}, u32[]{:S(2)}) collective-permute-start(bf16[272,256]{1,0:T(8,128)(2,1)S(1)} %collective-permute-done.3.refs_4_.refs_0_), channel_id=1, source_target_pairs={{1,0},{0,1},{3,2},{2,3},{5,4},{4,5},{7,6},{6,7},{9,8},{8,9},{11,10... | collective-permute-start | bytes 417800 | tf_op jit(solution)/shard_map/ppermute | solution.py:29
  16.9 5.2 %collective-permute-start = (bf16[272,256]{1,0:T(8,128)(2,1)S(1)}, bf16[272,256]{1,0:T(8,128)(2,1)S(1)}, u32[]{:S(2)}, u32[]{:S(2)}) collective-permute-start(bf16[272,256]{1,0:T(8,128)(2,1)S(1)} %get-tuple-element.6.refs_0_), channel_id=1, source_target_pairs={{4,0},{5,1},{6,2},{7,3},{0,4},{1,5},{2,6},{3,7},{12,8},{13,9},{14,... | collective-permute-start | bytes 417800 | tf_op jit(solution)/shard_map/ppermute | solution.py:29
  16.9 5.2 %collective-permute-start.2 = (bf16[272,256]{1,0:T(8,128)(2,1)S(1)}, bf16[272,256]{1,0:T(8,128)(2,1)S(1)}, u32[]{:S(2)}, u32[]{:S(2)}) collective-permute-start(bf16[272,256]{1,0:T(8,128)(2,1)S(1)} %collective-permute-done.1.refs_2_), channel_id=1, source_target_pairs={{4,0},{5,1},{6,2},{7,3},{0,4},{1,5},{2,6},{3,7},{12,8},{13,9},{14,... | collective-permute-start | bytes 417800 | tf_op jit(solution)/shard_map/ppermute | solution.py:29
  22.0 1.4 %collective-permute-start.9 = (bf16[8,64,128]{2,1,0:T(8,128)(2,1)S(1)}, bf16[8,64,128]{2,1,0:T(8,128)(2,1)S(1)}, u32[]{:S(2)}, u32[]{:S(2)}) collective-permute-start(bf16[8,64,128]{2,1,0:T(8,128)(2,1)S(1)} %picture.1), channel_id=1, source_target_pairs={{4,0},{5,1},{6,2},{7,3},{0,4},{1,5},{2,6},{3,7},{12,8},{13,9},{14,... | collective-permute-start | bytes 393224 | tf_op jit(solution)/shard_map/ppermute | solution.py:29
  23.4 5.8 %collective-permute-start.10 = (bf16[8,64,128]{2,1,0:T(8,128)(2,1)S(1)}, bf16[8,64,128]{2,1,0:T(8,128)(2,1)S(1)}, u32[]{:S(2)}, u32[]{:S(2)}) collective-permute-start(bf16[8,64,128]{2,1,0:T(8,128)(2,1)S(1)} %add_convert_fusion.refs_4_), channel_id=1, source_target_pairs={{12,0},{13,1},{14,2},{15,3},{8,4},{9,5},{10,6},{11,7},{4,8},{5,9},... | collective-permute-start | bytes 393224 | tf_op jit(solution)/shard_map/ppermute | solution.py:29
